TPU v7x, 32 devices: a whole 2x2x4 slice. The times are simulated.
32 devices in a mesh: seq: 2 (over core), pipe: 4 (over y, x), tp: 4 (over z).
Axes of the slice: x: 2, y: 2, z: 4, core: 2. Of those that a mesh axis runs over, the one named last changes fastest.
Arguments:
- queries: bfloat16 [4, 1024, 3072], P('pipe', 'seq', 'tp'), may hold values from -6 to 6
- keys: bfloat16 [4, 1024, 3072], P('pipe', 'seq', 'tp'), may hold values from -6 to 6
- values: bfloat16 [4, 1024, 3072], P('pipe', 'seq', 'tp'), may hold values from -6 to 6
- grad_out: bfloat16 [4, 1024, 3072], P('pipe', 'seq', 'tp'), may hold values from -6 to 6
- router: float32 [4, 1024], P('pipe', 'seq'), may hold values from 0.1 to 1
- blocks: int32 [4, 2, 3], P('pipe', 'seq'), may hold values from 0 to 3, as said below
- counts: int32 [4, 2], P('pipe', 'seq'), may hold values from 1 to 3, as said below
Outputs:
- section_grads: bfloat16 [4, 3, 768, 3072], P('pipe', None, 'seq', 'tp')
- router_grad: float32 [4, 768], P('pipe', 'seq')
Inputs may be any that keep to these rules, and one draw needn't show every extreme that they name: Per section and shard, the first counts entries are distinct block numbers in increasing order; the remaining entries are 0. In every draw some shard routes its last 3 blocks. `counts`: in every draw some shard routes 3 blocks and some routes 1.
All inputs are finite; a program needn't handle non-finite values.
Results may differ from a plain program's by a relative error of at most 0.0058.
Values may be sent and summed in bfloat16 or wider, within the bound.
No kernel may reach another device: no remote copies, remote signals or barrier semaphores. Data moves between devices by JAX's collectives and lax.ppermute only.
A program may use at most 128 MiB of HBM per device.

v0:
```python
import math
import jax
import jax.numpy as jnp
from jax import lax
from jax.sharding import PartitionSpec as P

HEAD_SIZE = 128
BLOCK_ROWS = 128


def carried_in(part, axis, combine, identity, reverse):
    count = lax.axis_size(axis)
    place = lax.axis_index(axis)
    ahead = count - 1 - place if reverse else place
    gathered = lax.all_gather(part, axis)
    state = jnp.zeros_like(part) + jnp.asarray(identity, part.dtype)

    def one(turn, state):
        source = count - 1 - turn if reverse else turn
        return combine(state, lax.dynamic_index_in_dim(gathered, source, 0, False))

    return lax.fori_loop(0, ahead, one, state)


def from_behind(x, axis, by):
    count = lax.axis_size(axis)
    return lax.ppermute(x, axis, [(i, (i + by) % count) for i in range(count)])


def plus_state(earlier, later):
    return earlier + later


def on_device(queries, keys, values, grad_out, router, blocks, counts):
    heads_dev = queries.shape[2] // HEAD_SIZE
    width_dev = queries.shape[2]
    slot_count = blocks.shape[2]
    shard_blocks = queries.shape[1] // BLOCK_ROWS
    seq_count = lax.axis_size("seq")
    factor = 1.0 / math.sqrt(HEAD_SIZE * slot_count * BLOCK_ROWS * seq_count)
    valid_slot = jnp.arange(slot_count, dtype=jnp.int32) < counts[0, 0]
    picker = (
        blocks[0, 0, :, None] == jnp.arange(shard_blocks, dtype=jnp.int32)[None, :]
    ) & valid_slot[:, None]
    picker_half = picker.astype(jnp.bfloat16)
    picker_full = picker.astype(jnp.float32)

    def select(array):
        grouped = array[0].reshape(shard_blocks, BLOCK_ROWS, width_dev)
        taken_blocks = jnp.einsum(
            "jb,btf->jtf", picker_half, grouped, preferred_element_type=jnp.float32
        ).astype(jnp.bfloat16)
        return taken_blocks.reshape(slot_count, BLOCK_ROWS, heads_dev, HEAD_SIZE)

    query_rows = select(queries)
    key_rows = select(keys)
    value_rows = select(values)
    grad_rows = select(grad_out)
    grad_wide = grad_rows.astype(jnp.float32)
    router_weight = jnp.einsum(
        "jb,bt->jt",
        picker_full,
        router[0].reshape(shard_blocks, BLOCK_ROWS),
        precision=lax.Precision.HIGHEST,
    )
    output_gradient = (router_weight.reshape(slot_count, BLOCK_ROWS, 1, 1) * grad_wide).astype(
        jnp.bfloat16
    )
    key_value = jnp.einsum(
        "nthd,nthe->nhde", key_rows, value_rows, preferred_element_type=jnp.float32
    )
    query_grad = jnp.einsum(
        "nthd,nthe->nhde", query_rows, output_gradient, preferred_element_type=jnp.float32
    )
    zero_state = jnp.zeros((1,) + key_value.shape[1:], jnp.float32)
    local_before = jnp.concatenate([zero_state, jnp.cumsum(key_value, axis=0)[:-1]], axis=0)
    flipped = jnp.flip(query_grad, axis=0)
    local_after = jnp.flip(
        jnp.concatenate([zero_state, jnp.cumsum(flipped, axis=0)[:-1]], axis=0), axis=0
    )
    shard_state = jnp.sum(key_value, axis=0)
    shard_grad = jnp.sum(query_grad, axis=0)
    empty_state = jnp.zeros_like(shard_state)
    earlier_state = carried_in(shard_state, "seq", plus_state, empty_state, False)
    later_grad = carried_in(shard_grad, "seq", plus_state, empty_state, True)
    before = (earlier_state[None] + local_before).astype(jnp.bfloat16)
    after = (later_grad[None] + local_after).astype(jnp.bfloat16)
    causal = jnp.arange(BLOCK_ROWS)[:, None] >= jnp.arange(BLOCK_ROWS)[None, :]
    grad_scores = jnp.where(
        causal,
        jnp.einsum(
            "nthe,nshe->nhts", output_gradient, value_rows, preferred_element_type=jnp.float32
        ),
        0.0,
    ).astype(jnp.bfloat16)
    scores = jnp.where(
        causal,
        jnp.einsum("nthd,nshd->nhts", query_rows, key_rows, preferred_element_type=jnp.float32),
        0.0,
    ).astype(jnp.bfloat16)
    output_core = factor * (
        jnp.einsum("nhts,nshe->nthe", scores, value_rows, preferred_element_type=jnp.float32)
        + jnp.einsum("nthd,nhde->nthe", query_rows, before, preferred_element_type=jnp.float32)
    )
    partial_router = jnp.sum(grad_wide * output_core, axis=(2, 3)).reshape(-1)
    router_grad = lax.psum(partial_router, "tp")
    query_gradient = factor * (
        jnp.einsum("nhts,nshd->nthd", grad_scores, key_rows, preferred_element_type=jnp.float32)
        + jnp.einsum("nthe,nhde->nthd", output_gradient, before, preferred_element_type=jnp.float32)
    )
    key_gradient = factor * (
        jnp.einsum("nhts,nthd->nshd", grad_scores, query_rows, preferred_element_type=jnp.float32)
        + jnp.einsum("nshe,nhde->nshd", value_rows, after, preferred_element_type=jnp.float32)
    )
    value_gradient = factor * (
        jnp.einsum("nhts,nthe->nshe", scores, output_gradient, preferred_element_type=jnp.float32)
        + jnp.einsum("nshd,nhde->nshe", key_rows, after, preferred_element_type=jnp.float32)
    )
    stacked_gradients = (
        jnp.stack([query_gradient, key_gradient, value_gradient])
        .reshape(1, 3, slot_count * BLOCK_ROWS, heads_dev * HEAD_SIZE)
        .astype(jnp.bfloat16)
    )
    handed = from_behind(stacked_gradients, "pipe", -1)
    return (handed, router_grad.reshape(1, slot_count * BLOCK_ROWS))


def solution(mesh):
    return jax.shard_map(
        on_device,
        mesh=mesh,
        in_specs=(
            P("pipe", "seq", "tp"),
            P("pipe", "seq", "tp"),
            P("pipe", "seq", "tp"),
            P("pipe", "seq", "tp"),
            P("pipe", "seq"),
            P("pipe", "seq", None),
            P("pipe", "seq"),
        ),
        out_specs=(P("pipe", None, "seq", "tp"), P("pipe", "seq")),
        check_vma=False,
    )
```

profile of v0, /device:TPU:0, one launch (start us, length us, event | category | flops | bytes accessed | tf_op | source)
XLA Modules:
  0.0 111.4 jit_solution(18025959512974319276)
XLA Ops:
  0.6 0.0 copy-start
  1.4 0.7 fusion.20
  2.1 0.0 copy-done
  2.1 0.7 fusion.6
  2.8 0.0 copy-start.8
  2.8 1.5 %copy.58 = f32[3,128,768]{1,2,0:T(8,128)} copy(f32[3,128,768]{2,0,1:T(4,128)S(1)} %fusion.6) | data formatting | bytes 2359296 | tf_op jit(solution)/shard_map/convert_element_type | solution.py:59
  4.3 0.0 copy-done.8
  4.3 0.1 fusion.31
  4.4 1.8 %convolution_convert_fusion = bf16[3,128,768]{2,0,1:T(4,128)(2,1)S(1)} fusion(bf16[4,128,768]{2,1,0:T(8,128)(2,1)} %bitcast.94, pred[3,4]{1,0:T(4,128)(4,1)S(1)} %fusion.20), kind=kOutput, calls=%fused_computation.12 | convolution fusion | flops 2654208 | bytes 1376268 | tf_op jit(solution)/shard_map/jb,btf->jtf/dot_general | solution.py:50
  6.3 0.6 copy.67
  6.9 1.8 %convolution_convert_fusion.3 = bf16[3,128,768]{2,0,1:T(4,128)(2,1)S(1)} fusion(bf16[4,128,768]{2,1,0:T(8,128)(2,1)} %bitcast.95, pred[3,4]{1,0:T(4,128)(4,1)S(1)} %fusion.20), kind=kOutput, calls=%fused_computation.19 | convolution fusion | flops 2654208 | bytes 1376268 | tf_op jit(solution)/shard_map/jb,btf->jtf/dot_general | solution.py:50
  8.8 0.6 copy.56
  9.4 2.7 %convolution_convert_fusion.1 = bf16[3,128,768]{2,0,1:T(4,128)(2,1)} fusion(bf16[4,128,768]{2,1,0:T(8,128)(2,1)} %bitcast.96, pred[3,4]{1,0:T(4,128)(4,1)S(1)} %fusion.20), kind=kOutput, calls=%fused_computation.16 | convolution fusion | flops 2654208 | bytes 1376268 | tf_op jit(solution)/shard_map/jb,btf->jtf/dot_general | solution.py:50
  12.1 1.5 %copy.60 = bf16[3,128,768]{1,2,0:T(8,128)(2,1)S(1)} copy(bf16[3,128,768]{2,0,1:T(4,128)(2,1)} %convolution_convert_fusion.1) | data formatting | bytes 1179648 | tf_op jit(solution)/shard_map/convert_element_type | solution.py:52
  13.6 1.4 %multiply_convert_fusion = bf16[3,128,6,128]{1,3,2,0:T(8,128)(2,1)S(1)} fusion(f32[3,128,6,128]{1,3,2,0:T(8,128)} %bitcast.87, f32[3,128]{1,0:T(4,128)S(1)} %fusion.31), kind=kLoop, calls=%fused_computation.31 | loop fusion | flops 589824 | bytes 1771008 | tf_op jit(solution)/shard_map/convert_element_type | solution.py:66
  15.0 1.6 %fusion.27 = (f32[6,128,128]{2,1,0:T(8,128)S(1)}, f32[3,6,128,128]{3,2,1,0:T(8,128)}) fusion(bf16[3,128,6,128]{1,3,2,0:T(8,128)(2,1)S(1)} %bitcast.75, bf16[3,128,6,128]{1,3,2,0:T(8,128)(2,1)S(1)} %multiply_convert_fusion), kind=kOutput, calls=%fused_computation.47 | convolution fusion | flops 75694080 | bytes 2752512 | tf_op jit(solution)/shard_map/nthd,nthe->nhde/dot_general | solution.py:72
  16.6 1.2 %fusion.10 = bf16[3,6,128,128]{3,2,1,0:T(8,128)(2,1)} fusion(bf16[3,128,6,128]{1,3,2,0:T(8,128)(2,1)S(1)} %bitcast.76, bf16[3,128,6,128]{1,3,2,0:T(8,128)(2,1)S(1)} %bitcast.83, pred[128,128]{1,0:T(8,128)(4,1)S(1)} %iota_compare_fusion), kind=kOutput, calls=%fused_computation.23 | convolution fusion | flops 76087296 | bytes 1785856 | tf_op jit(solution)/shard_map/nthd,nshd->nhts/dot_general | solution.py:98
  17.8 0.4 fusion.7
  18.2 1.3 %fusion.33 = f32[3,6,128,128]{3,2,1,0:T(8,128)} fusion(bf16[3,128,6,128]{1,3,2,0:T(8,128)(2,1)S(1)} %bitcast.77, bf16[3,6,128,128]{3,2,1,0:T(8,128)(2,1)S(1)} %fusion.7), kind=kOutput, calls=%fused_computation.53 | convolution fusion | flops 75497472 | bytes 2359296 | tf_op jit(solution)/shard_map/nhts,nthd->nshd/dot_general | solution.py:112
  19.5 1.5 %fusion.32 = f32[3,6,128,128]{3,2,1,0:T(8,128)} fusion(bf16[3,128,6,128]{1,3,2,0:T(8,128)(2,1)S(1)} %bitcast.84, bf16[3,6,128,128]{3,2,1,0:T(8,128)(2,1)S(1)} %fusion.7), kind=kOutput, calls=%fused_computation.52 | convolution fusion | flops 75497472 | bytes 2359296 | tf_op jit(solution)/shard_map/nhts,nshd->nthd/dot_general | solution.py:108
  21.1 2.4 %fusion.28 = (f32[6,128,128]{2,1,0:T(8,128)}, f32[3,6,128,128]{3,2,1,0:T(8,128)}) fusion(bf16[3,128,6,128]{1,3,2,0:T(8,128)(2,1)S(1)} %bitcast.85, bf16[3,128,6,128]{1,3,2,0:T(8,128)(2,1)S(1)} %bitcast.80), kind=kOutput, calls=%fused_computation.48 | convolution fusion | flops 75694080 | bytes 2752512 | tf_op jit(solution)/shard_map/nthd,nthe->nhde/dot_general | solution.py:69
  23.4 2.4 %fusion.34 = f32[3,6,128,128]{3,2,1,0:T(8,128)} fusion(bf16[3,128,6,128]{1,3,2,0:T(8,128)(2,1)S(1)} %multiply_convert_fusion, bf16[3,6,128,128]{3,2,1,0:T(8,128)(2,1)} %fusion.10), kind=kOutput, calls=%fused_computation.54 | convolution fusion | flops 75497472 | bytes 2359296 | tf_op jit(solution)/shard_map/nhts,nthe->nshe/dot_general | solution.py:116
  25.8 2.4 %rev.7 = f32[3,6,128,128]{3,2,1,0:T(8,128)} reverse(f32[3,6,128,128]{3,2,1,0:T(8,128)} %get-tuple-element.100), dimensions={0} | reverse | bytes 2359296 | tf_op jit(solution)/shard_map/jit(_flip)/rev | solution.py:77
  28.2 1.4 %fusion.30 = f32[3,6,128,128]{3,2,1,0:T(8,128)S(1)} fusion(f32[3,6,128,128]{3,2,1,0:T(8,128)} %rev.7), kind=kOutput, calls=%fused_computation.50 | output fusion | flops 589824 | bytes 2359296 | tf_op jit(solution)/shard_map/jit(cumsum)/reduce_window_sum | solution.py:79
  29.6 1.0 slice.9
  30.6 2.6 %all-gather.1 = f32[12,128,128]{2,1,0:T(8,128)} all-gather(f32[6,128,128]{2,1,0:T(8,128)S(1)} %get-tuple-element.99), channel_id=3, replica_groups=mesh['seq'=2,'pipe'=4,'tp'=4] {'seq'}, dimensions={0}, use_global_device_ids=true | all-gather | bytes 1179648 | tf_op jit(solution)/shard_map/all_gather | solution.py:15
  33.2 1.1 %while.23 = (s32[]{:T(128)}, f32[6,128,128]{2,1,0:T(8,128)S(1)}, s32[]{:T(128)}, f32[2,6,128,128]{3,2,1,0:T(8,128)}, s32[]{:T(128)}, /*index=5*/s32[]{:T(128)}, s32[]{:T(128)}) while((s32[]{:T(128)}, f32[6,128,128]{2,1,0:T(8,128)S(1)}, s32[]{:T(128)}, f32[2,6,128,128]{3,2,1,0:T(8,128)}, s32[]{:T(128)}, /*index=5*/s32[]{:T(128)}, ...), condition=%wide.region_6.7_spmd, body=%wide.region_5.6_spmd.sunk | while | flops 98310 | bytes 1179783 | solution.py:22
  33.2 1.1 bitcast_add_fusion.5
  34.3 1.2 %concatenate.16 = f32[3,6,128,128]{3,2,1,0:T(8,128)S(1)} pad(f32[2,6,128,128]{3,2,1,0:T(8,128)} %slice.9, f32[]{:T(128)} %constant.41.clone.1), padding=1_0x0_0x0_0x0_0 | pad | bytes 1966084 | tf_op jit(solution)/shard_map/concatenate | solution.py:79
  35.6 0.0 copy-start.6
  35.6 0.1 add_convert_fusion
  35.7 0.0 copy-start.4
  35.7 0.8 copy-done.4
  36.6 0.5 copy-done.6
  37.1 1.2 %fusion.13 = bf16[3,128,6,128]{1,3,2,0:T(8,128)(2,1)} fusion(f32[3,6,128,128]{3,2,1,0:T(8,128)S(1)} %copy-done.6, bf16[3,6,128,128]{3,2,1,0:T(8,128)(2,1)S(1)} %add_convert_fusion, bf16[3,128,6,128]{1,3,2,0:T(8,128)(2,1)S(1)} %bitcast.86), kind=kOutput, calls=%fused_computation.26 | convolution fusion | flops 76382208 | bytes 2949120 | tf_op jit(solution)/shard_map/nshd,nhde->nshe/dot_general | solution.py:117
  38.3 0.0 copy-start.5
  38.3 2.4 %copy.75 = bf16[3,128,6,128]{3,2,1,0:T(8,128)(2,1)} copy(bf16[3,128,6,128]{1,3,2,0:T(8,128)(2,1)} %fusion.13) | data formatting | bytes 1179648 | tf_op jit(solution)/shard_map/mul | solution.py:115
  40.7 2.5 %stack.14 = bf16[1,1,384,768]{3,2,1,0:T(8,128)(2,1)} reshape(bf16[3,128,6,128]{3,2,1,0:T(8,128)(2,1)} %copy.75) | data formatting | bytes 1179648 | tf_op jit(solution)/shard_map/stack | solution.py:120
  43.1 0.0 copy-done.5
  43.1 2.4 %fusion.14 = bf16[3,128,6,128]{1,3,2,0:T(8,128)(2,1)} fusion(f32[3,6,128,128]{3,2,1,0:T(8,128)} %fusion.33, bf16[3,6,128,128]{3,2,1,0:T(8,128)(2,1)S(1)} %copy-done.5, bf16[3,128,6,128]{1,3,2,0:T(8,128)(2,1)S(1)} %bitcast.81), kind=kOutput, calls=%fused_computation.27 | convolution fusion | flops 76382208 | bytes 2949120 | tf_op jit(solution)/shard_map/nshe,nhde->nshd/dot_general | solution.py:113
  45.5 2.3 %copy.70 = bf16[3,128,6,128]{3,2,1,0:T(8,128)(2,1)} copy(bf16[3,128,6,128]{1,3,2,0:T(8,128)(2,1)} %fusion.14) | data formatting | bytes 1179648 | tf_op jit(solution)/shard_map/mul | solution.py:111
  47.8 2.5 %stack.13 = bf16[1,1,384,768]{3,2,1,0:T(8,128)(2,1)} reshape(bf16[3,128,6,128]{3,2,1,0:T(8,128)(2,1)} %copy.70) | data formatting | bytes 1179648 | tf_op jit(solution)/shard_map/stack | solution.py:120
  50.3 1.4 %fusion.29 = f32[3,6,128,128]{3,2,1,0:T(8,128)S(1)} fusion(f32[3,6,128,128]{3,2,1,0:T(8,128)} %get-tuple-element.102), kind=kOutput, calls=%fused_computation.49 | output fusion | flops 589824 | bytes 2359296 | tf_op jit(solution)/shard_map/jit(cumsum)/reduce_window_sum | solution.py:76
  51.7 0.0 copy-start.7
  51.7 0.9 slice.8
  52.6 0.1 copy-done.7
  52.7 2.5 %all-gather = f32[12,128,128]{2,1,0:T(8,128)} all-gather(f32[6,128,128]{2,1,0:T(8,128)S(1)} %copy-done.7), channel_id=2, replica_groups=mesh['seq'=2,'pipe'=4,'tp'=4] {'seq'}, dimensions={0}, use_global_device_ids=true | all-gather | bytes 1179648 | tf_op jit(solution)/shard_map/all_gather | solution.py:15
  55.3 0.2 while.22
  55.5 2.6 %fusion.15 = bf16[3,128,6,128]{1,3,2,0:T(8,128)(2,1)} fusion(f32[3,6,128,128]{3,2,1,0:T(8,128)} %fusion.32, bf16[3,128,6,128]{1,3,2,0:T(8,128)(2,1)S(1)} %multiply_convert_fusion, f32[2,6,128,128]{3,2,1,0:T(8,128)} %slice.8, f32[6,128,128]{2,1,0:T(8,128)S(1)} %get-tuple-element.81), kind=kOutput, calls=%fused_computation.28 | convolution fusion | flops 76972032 | bytes 3538944 | tf_op jit(solution)/shard_map/nthe,nhde->nthd/dot_general | solution.py:109
  58.1 2.3 %copy.65 = bf16[3,128,6,128]{3,2,1,0:T(8,128)(2,1)} copy(bf16[3,128,6,128]{1,3,2,0:T(8,128)(2,1)} %fusion.15) | data formatting | bytes 1179648 | tf_op jit(solution)/shard_map/mul | solution.py:107
  60.4 2.5 %stack.12 = bf16[1,1,384,768]{3,2,1,0:T(8,128)(2,1)} reshape(bf16[3,128,6,128]{3,2,1,0:T(8,128)(2,1)} %copy.65) | data formatting | bytes 1179648 | tf_op jit(solution)/shard_map/stack | solution.py:120
  62.9 0.0 copy-start.3
  62.9 2.9 %pad_maximum_fusion = bf16[1,3,384,768]{3,2,1,0:T(8,128)(2,1)} fusion(bf16[1,1,384,768]{3,2,1,0:T(8,128)(2,1)} %stack.14, bf16[1,1,384,768]{3,2,1,0:T(8,128)(2,1)} %stack.13, bf16[1,1,384,768]{3,2,1,0:T(8,128)(2,1)} %stack.12), kind=kLoop, calls=%fused_computation.2 | loop fusion | flops 1769472 | bytes 3538944 | tf_op jit(solution)/shard_map/stack | solution.py:120
  65.7 0.0 copy-start.1
  65.7 0.0 copy-start.2
  65.7 3.8 %collective-permute-start = (bf16[1,3,384,768]{3,2,1,0:T(8,128)(2,1)}, bf16[1,3,384,768]{3,2,1,0:T(8,128)(2,1)}, u32[]{:S(2)}, u32[]{:S(2)}) collective-permute-start(bf16[1,3,384,768]{3,2,1,0:T(8,128)(2,1)} %pad_maximum_fusion), channel_id=1, source_target_pairs={{0,12},{4,0},{8,4},{12,8},{1,13},{5,1},{9,5},{13,9},{2,14},{6,2},{... | collective-permute-start | bytes 5308424 | tf_op jit(solution)/shard_map/ppermute | solution.py:27
  69.6 0.0 copy-done.3
  69.6 0.5 fusion.35
  70.1 0.0 copy-done.1
  70.1 0.0 copy-done.2
  70.1 0.5 fusion.12
  70.6 12.6 %psum.7 = f32[1,384]{1,0:T(1,128)} all-reduce(f32[1,384]{1,0:T(1,128)S(1)} %bitcast.92), channel_id=1, replica_groups=mesh['seq'=2,'pipe'=4,'tp'=4] {'tp'}, use_global_device_ids=true, to_apply=%region_9.10 | all-reduce | flops 384 | bytes 3072 | tf_op jit(solution)/shard_map/psum | solution.py:106
  83.2 25.4 %collective-permute-done = bf16[1,3,384,768]{3,2,1,0:T(8,128)(2,1)} collective-permute-done((bf16[1,3,384,768]{3,2,1,0:T(8,128)(2,1)}, bf16[1,3,384,768]{3,2,1,0:T(8,128)(2,1)}, u32[]{:S(2)}, u32[]{:S(2)}) %collective-permute-start) | collective-permute-done | bytes 1769504 | tf_op jit(solution)/shard_map/ppermute | solution.py:27
  108.6 2.8 %copy.116 = bf16[1,3,384,768]{3,2,1,0:T(8,128)(2,1)} copy(bf16[1,3,384,768]{3,2,1,0:T(8,128)(2,1)} %collective-permute-done) | data formatting | bytes 3538944
  (5 shorter events, 0.1 us)
Async XLA Ops:
  0.6 1.5 %copy-start = (bf16[1,512,768]{2,1,0:T(8,128)(2,1)S(1)}, bf16[1,512,768]{2,1,0:T(8,128)(2,1)}, u32[]{:S(2)}) copy-start(bf16[1,512,768]{2,1,0:T(8,128)(2,1)} %param.14) | copy-start | bytes 2359300
  2.8 1.5 %copy-start.8 = (f32[1,512]{1,0:T(1,128)S(1)}, f32[1,512]{1,0:T(1,128)}, u32[]{:S(2)}) copy-start(f32[1,512]{1,0:T(1,128)} %param.15) | copy-start | bytes 6148
  35.6 1.5 %copy-start.6 = (f32[3,6,128,128]{3,2,1,0:T(8,128)S(1)}, f32[3,6,128,128]{3,2,1,0:T(8,128)}, u32[]{:S(2)}) copy-start(f32[3,6,128,128]{3,2,1,0:T(8,128)} %fusion.34) | copy-start | bytes 3538948
  35.7 0.8 copy-start.4
  38.3 4.8 %copy-start.5 = (bf16[3,6,128,128]{3,2,1,0:T(8,128)(2,1)S(1)}, bf16[3,6,128,128]{3,2,1,0:T(8,128)(2,1)}, u32[]{:S(2)}) copy-start(bf16[3,6,128,128]{3,2,1,0:T(8,128)(2,1)} %copy-done.4) | copy-start | bytes 1769476
  51.7 1.1 copy-start.7
  62.9 6.7 %copy-start.3 = (bf16[3,6,128,128]{3,2,1,0:T(8,128)(2,1)S(1)}, bf16[3,6,128,128]{3,2,1,0:T(8,128)(2,1)}, u32[]{:S(2)}) copy-start(bf16[3,6,128,128]{3,2,1,0:T(8,128)(2,1)} %fusion.10) | copy-start | bytes 1769476
  65.7 4.4 %copy-start.1 = (f32[3,128,768]{1,2,0:T(8,128)S(1)}, f32[3,128,768]{1,2,0:T(8,128)}, u32[]{:S(2)}) copy-start(f32[3,128,768]{1,2,0:T(8,128)} %copy.58) | copy-start | bytes 3538948
  65.7 4.4 %copy-start.2 = (f32[2,6,128,128]{3,2,1,0:T(8,128)S(1)}, f32[2,6,128,128]{3,2,1,0:T(8,128)}, u32[]{:S(2)}) copy-start(f32[2,6,128,128]{3,2,1,0:T(8,128)} %slice.8) | copy-start | bytes 2359300
  65.7 42.8 %collective-permute-start = (bf16[1,3,384,768]{3,2,1,0:T(8,128)(2,1)}, bf16[1,3,384,768]{3,2,1,0:T(8,128)(2,1)}, u32[]{:S(2)}, u32[]{:S(2)}) collective-permute-start(bf16[1,3,384,768]{3,2,1,0:T(8,128)(2,1)} %pad_maximum_fusion), channel_id=1, source_target_pairs={{0,12},{4,0},{8,4},{12,8},{1,13},{5,1},{9,5},{13,9},{2,14},{6,2},{... | collective-permute-start | bytes 5308424 | tf_op jit(solution)/shard_map/ppermute | solution.py:27
where the time goes:
time: 112 us; the launch traced here: 111 us
  local copies, waits for them, and re-layouts  28.5 us (25%)
  waiting for transfers between devices  25.4 us (23%)
  matrix products  25.3 us (23%)
  blocking collectives  17.7 us (16%)
  other arithmetic  8.97 us (8%)
  starting transfers between devices  3.82 us (3%)
  between operations  1.55 us (1%)
    ppermute x1, waiting for transfers between devices, from_behind(): return lax.ppermute(x, axis, [(i, (i + by) % count) for i in range(count)])  25.4 us
    psum x1, blocking collectives, on_device(): router_grad = lax.psum(partial_router, 'tp')  12.6 us
    another operation x3, local copies, waits for them, and re-layouts, on_device(): jnp.stack([query_gradient, key_gradient, value_gradient])  7.38 us
    dot_general x4, matrix products, select(): jnp.einsum('jb,btf->jtf', picker_half, grouped, preferred_element_type=jn...  7.09 us
    all_gather x2, blocking collectives, carried_in(): gathered = lax.all_gather(part, axis)  5.1 us
    unnamed x20, local copies, waits for them, and re-layouts  4.28 us
    ppermute x1, starting transfers between devices, from_behind(): return lax.ppermute(x, axis, [(i, (i + by) % count) for i in range(count)])  3.82 us
    another operation x1, other arithmetic, on_device(): jnp.stack([query_gradient, key_gradient, value_gradient])  2.88 us
  transfers between devices with their start and end apart: 1, of which 1 were waited for; matrix products, arithmetic and copies ran while one was open for 1% of the time, Pallas kernels for 0%

commit v1 on v0

--- a/solution.py
+++ b/solution.py
@@ -6,6 +6,14 @@
 
 HEAD_SIZE = 128
 BLOCK_ROWS = 128
+
+
+def added_up(x, name):
+    size, total = (lax.axis_size(name), x)
+    for reach in [1 << k for k in range(size.bit_length() - 1)]:
+        route = [(i, i ^ reach) for i in range(size)]
+        total = total + lax.ppermute(total, name, route)
+    return total
 
 
 def carried_in(part, axis, combine, identity, reverse):
@@ -103,7 +111,7 @@
         + jnp.einsum("nthd,nhde->nthe", query_rows, before, preferred_element_type=jnp.float32)
     )
     partial_router = jnp.sum(grad_wide * output_core, axis=(2, 3)).reshape(-1)
-    router_grad = lax.psum(partial_router, "tp")
+    router_grad = added_up(partial_router, "tp")
     query_gradient = factor * (
         jnp.einsum("nhts,nshd->nthd", grad_scores, key_rows, preferred_element_type=jnp.float32)
         + jnp.einsum("nthe,nhde->nthd", output_gradient, before, preferred_element_type=jnp.float32)

time: 112 us -> 104 us (0.929)
  blocking collectives: 17.7 us -> 6.2 us
  waiting for transfers between devices: 25.4 us -> 31.4 us
  starting transfers between devices: 3.82 us -> 7.86 us
  matrix products: 25.3 us -> 22.1 us
  other arithmetic: 8.97 us -> 6.27 us
    psum x1 -> x0, blocking collectives: 12.6 us -> none  [on_device(): router_grad = lax.psum(partial_router, 'tp')]
    ppermute x0 -> x2, starting transfers between devices: none -> 4.25 us  [added_up(): total = total + lax.ppermute(total, name, route)]
    ppermute x0 -> x2, waiting for transfers between devices: none -> 3.88 us  [added_up(): total = total + lax.ppermute(total, name, route)]
    ppermute x1, waiting for transfers between devices: 25.4 us -> 27.6 us  [from_behind(): return lax.ppermute(x, axis, [(i, (i + by) % count) for i in range(count)])]
    dot_general x1, matrix products: 2.39 us -> 0.31 us  [on_device(): jnp.einsum('nhts,nthe->nshe', scores, output_gradient, preferred_element_...]
    another operation x1, other arithmetic: 2.88 us -> 1.43 us  [on_device(): jnp.stack([query_gradient, key_gradient, value_gradient])]
    dot_general x1, matrix products: 2.42 us -> 1.14 us  [on_device(): jnp.einsum('nshe,nhde->nshd', value_rows, after, preferred_element_type=j...]
    convert_element_type x1, other arithmetic: 1.41 us -> 0.14 us  [on_device(): (router_weight.reshape(slot_count, BLOCK_ROWS, 1, 1) * grad_wide).astype(...]
  transfers between devices with their start and end apart: 1 -> 3, of which waited for: 1 -> 3; matrix products, arithmetic and copies ran while one was open for 1% -> 2% of each run, Pallas kernels for 0% -> 0%
where the time goes in v1:
time: 104 us; the launch traced here: 103 us
  waiting for transfers between devices  31.4 us (30%)
  local copies, waits for them, and re-layouts  27.4 us (26%)
  matrix products  22.1 us (21%)
  starting transfers between devices  7.86 us (8%)
  other arithmetic  6.27 us (6%)
  blocking collectives  6.2 us (6%)
  between operations  1.59 us (2%)
    ppermute x1, waiting for transfers between devices, from_behind(): return lax.ppermute(x, axis, [(i, (i + by) % count) for i in range(count)])  27.6 us
    another operation x3, local copies, waits for them, and re-layouts, on_device(): jnp.stack([query_gradient, key_gradient, value_gradient])  7.39 us
    dot_general x4, matrix products, select(): jnp.einsum('jb,btf->jtf', picker_half, grouped, preferred_element_type=jn...  7.32 us
    all_gather x2, blocking collectives, carried_in(): gathered = lax.all_gather(part, axis)  6.2 us
    ppermute x2, starting transfers between devices, added_up(): total = total + lax.ppermute(total, name, route)  4.25 us
    ppermute x2, waiting for transfers between devices, added_up(): total = total + lax.ppermute(total, name, route)  3.88 us
    unnamed x29, local copies, waits for them, and re-layouts  3.65 us
    ppermute x1, starting transfers between devices, from_behind(): return lax.ppermute(x, axis, [(i, (i + by) % count) for i in range(count)])  3.61 us
  transfers between devices with their start and end apart: 3, of which 3 were waited for; matrix products, arithmetic and copies ran while one was open for 2% of the time, Pallas kernels for 0%

profile of v1, /device:TPU:0, one launch (start us, length us, event | category | flops | bytes accessed | tf_op | source)
XLA Modules:
  0.0 103.1 jit_solution(5011562606722356653)
XLA Ops:
  0.6 0.0 copy-start
  1.4 0.7 fusion.20
  2.1 0.0 copy-done
  2.1 0.7 convolution_convert_fusion
  2.8 0.6 copy.67
  3.5 1.8 %convolution_convert_fusion.3 = bf16[3,128,768]{2,0,1:T(4,128)(2,1)S(1)} fusion(bf16[4,128,768]{2,1,0:T(8,128)(2,1)} %bitcast.91, pred[3,4]{1,0:T(4,128)(4,1)S(1)} %fusion.20), kind=kOutput, calls=%fused_computation.19 | convolution fusion | flops 2654208 | bytes 1376268 | tf_op jit(solution)/shard_map/jb,btf->jtf/dot_general | solution.py:58
  5.3 0.6 copy.56
  5.9 0.0 copy-start.1
  5.9 0.0 copy-start.12
  5.9 2.9 %convolution_convert_fusion.1 = bf16[3,128,768]{2,0,1:T(4,128)(2,1)} fusion(bf16[4,128,768]{2,1,0:T(8,128)(2,1)} %bitcast.92, pred[3,4]{1,0:T(4,128)(4,1)S(1)} %fusion.20), kind=kOutput, calls=%fused_computation.16 | convolution fusion | flops 2654208 | bytes 1376268 | tf_op jit(solution)/shard_map/jb,btf->jtf/dot_general | solution.py:58
  8.9 1.5 %copy.60 = bf16[3,128,768]{1,2,0:T(8,128)(2,1)S(1)} copy(bf16[3,128,768]{2,0,1:T(4,128)(2,1)} %convolution_convert_fusion.1) | data formatting | bytes 1179648 | tf_op jit(solution)/shard_map/convert_element_type | solution.py:60
  10.4 0.0 copy-done.12
  10.4 1.8 %fusion.6 = f32[3,128,768]{2,0,1:T(4,128)} fusion(bf16[4,128,768]{2,1,0:T(8,128)(2,1)S(1)} %bitcast.88, pred[3,4]{1,0:T(4,128)(4,1)S(1)} %fusion.20), kind=kOutput, calls=%fused_computation.18 | convolution fusion | flops 2949120 | bytes 1966092 | tf_op jit(solution)/shard_map/jb,btf->jtf/dot_general | solution.py:58
  12.3 2.4 %copy.58 = f32[3,128,768]{1,2,0:T(8,128)} copy(f32[3,128,768]{2,0,1:T(4,128)} %fusion.6) | data formatting | bytes 2359296 | tf_op jit(solution)/shard_map/convert_element_type | solution.py:67
  14.7 0.1 fusion.31
  14.8 1.6 %fusion.28 = (f32[6,128,128]{2,1,0:T(8,128)S(1)}, f32[3,6,128,128]{3,2,1,0:T(8,128)}) fusion(bf16[3,128,6,128]{1,3,2,0:T(8,128)(2,1)S(1)} %bitcast.80, bf16[3,128,6,128]{1,3,2,0:T(8,128)(2,1)S(1)} %bitcast.76), kind=kOutput, calls=%fused_computation.48 | convolution fusion | flops 75694080 | bytes 2752512 | tf_op jit(solution)/shard_map/nthd,nthe->nhde/dot_general | solution.py:77
  16.4 1.2 %fusion.10 = bf16[3,6,128,128]{3,2,1,0:T(8,128)(2,1)} fusion(bf16[3,128,6,128]{1,3,2,0:T(8,128)(2,1)S(1)} %bitcast.72, bf16[3,128,6,128]{1,3,2,0:T(8,128)(2,1)S(1)} %bitcast.81, pred[128,128]{1,0:T(8,128)(4,1)S(1)} %iota_compare_fusion), kind=kOutput, calls=%fused_computation.23 | convolution fusion | flops 76087296 | bytes 1785856 | tf_op jit(solution)/shard_map/nthd,nshd->nhts/dot_general | solution.py:106
  17.6 0.1 copy-done.3
  17.7 0.1 multiply_convert_fusion
  17.8 2.3 %fusion.27 = (f32[6,128,128]{2,1,0:T(8,128)}, f32[3,6,128,128]{3,2,1,0:T(8,128)}) fusion(bf16[3,128,6,128]{1,3,2,0:T(8,128)(2,1)S(1)} %bitcast.73, bf16[3,128,6,128]{1,3,2,0:T(8,128)(2,1)S(1)} %multiply_convert_fusion), kind=kOutput, calls=%fused_computation.47 | convolution fusion | flops 75694080 | bytes 2752512 | tf_op jit(solution)/shard_map/nthd,nthe->nhde/dot_general | solution.py:80
  20.1 0.4 fusion.7
  20.5 1.3 %fusion.33 = f32[3,6,128,128]{3,2,1,0:T(8,128)} fusion(bf16[3,128,6,128]{1,3,2,0:T(8,128)(2,1)S(1)} %bitcast.74, bf16[3,6,128,128]{3,2,1,0:T(8,128)(2,1)S(1)} %fusion.7), kind=kOutput, calls=%fused_computation.53 | convolution fusion | flops 75497472 | bytes 2359296 | tf_op jit(solution)/shard_map/nhts,nthd->nshd/dot_general | solution.py:120
  21.9 0.0 copy-done.1
  21.9 1.5 %fusion.32 = f32[3,6,128,128]{3,2,1,0:T(8,128)} fusion(bf16[3,128,6,128]{1,3,2,0:T(8,128)(2,1)S(1)} %bitcast.82, bf16[3,6,128,128]{3,2,1,0:T(8,128)(2,1)S(1)} %fusion.7), kind=kOutput, calls=%fused_computation.52 | convolution fusion | flops 75497472 | bytes 2359296 | tf_op jit(solution)/shard_map/nhts,nshd->nthd/dot_general | solution.py:116
  23.4 2.6 %all-gather = f32[12,128,128]{2,1,0:T(8,128)} all-gather(f32[6,128,128]{2,1,0:T(8,128)S(1)} %get-tuple-element.101), channel_id=2, replica_groups=mesh['seq'=2,'pipe'=4,'tp'=4] {'seq'}, dimensions={0}, use_global_device_ids=true | all-gather | bytes 1179648 | tf_op jit(solution)/shard_map/all_gather | solution.py:23
  26.1 1.4 %fusion.29 = f32[3,6,128,128]{3,2,1,0:T(8,128)S(1)} fusion(f32[3,6,128,128]{3,2,1,0:T(8,128)} %get-tuple-element.102), kind=kOutput, calls=%fused_computation.49 | output fusion | flops 589824 | bytes 2359296 | tf_op jit(solution)/shard_map/jit(cumsum)/reduce_window_sum | solution.py:84
  27.4 1.0 slice.8
  28.4 0.1 copy-done.11
  28.5 3.6 %all-gather.1 = f32[12,128,128]{2,1,0:T(8,128)} all-gather(f32[6,128,128]{2,1,0:T(8,128)S(1)} %copy-done.11), channel_id=3, replica_groups=mesh['seq'=2,'pipe'=4,'tp'=4] {'seq'}, dimensions={0}, use_global_device_ids=true | all-gather | bytes 1179648 | tf_op jit(solution)/shard_map/all_gather | solution.py:23
  32.1 1.3 %while.23 = (s32[]{:T(128)}, f32[6,128,128]{2,1,0:T(8,128)S(1)}, s32[]{:T(128)}, f32[2,6,128,128]{3,2,1,0:T(8,128)}, s32[]{:T(128)}, /*index=5*/s32[]{:T(128)}, s32[]{:T(128)}) while((s32[]{:T(128)}, f32[6,128,128]{2,1,0:T(8,128)S(1)}, s32[]{:T(128)}, f32[2,6,128,128]{3,2,1,0:T(8,128)}, s32[]{:T(128)}, /*index=5*/s32[]{:T(128)}, ...), condition=%wide.region_6.7_spmd, body=%wide.region_5.6_spmd.sunk | while | flops 98310 | bytes 1179775 | solution.py:30
  32.2 1.1 %bitcast_add_fusion.6 = f32[6,128,128]{2,1,0:T(8,128)S(1)} fusion(f32[6,128,128]{2,1,0:T(8,128)S(1)} %get-tuple-element.163, f32[2,6,128,128]{3,2,1,0:T(8,128)} %get-tuple-element.172, s32[]{:T(128)S(6)} %select_n.29), kind=kLoop, calls=%fused_computation.1.clone.1 | loop fusion | flops 98304 | bytes 1179652 | tf_op jit(solution)/shard_map/while/body/add | solution.py:39
  33.4 2.4 %rev.7 = f32[3,6,128,128]{3,2,1,0:T(8,128)} reverse(f32[3,6,128,128]{3,2,1,0:T(8,128)} %get-tuple-element.100), dimensions={0} | reverse | bytes 2359296 | tf_op jit(solution)/shard_map/jit(_flip)/rev | solution.py:85
  35.8 1.4 %fusion.30 = f32[3,6,128,128]{3,2,1,0:T(8,128)S(1)} fusion(f32[3,6,128,128]{3,2,1,0:T(8,128)} %rev.7), kind=kOutput, calls=%fused_computation.50 | output fusion | flops 589824 | bytes 2359296 | tf_op jit(solution)/shard_map/jit(cumsum)/reduce_window_sum | solution.py:87
  37.2 0.1 slice.9
  37.3 0.1 concatenate.16
  37.4 0.1 add_convert_fusion
  37.5 0.8 copy-done.7
  38.3 0.5 copy-done.9
  38.8 1.1 %fusion.14 = bf16[3,128,6,128]{1,3,2,0:T(8,128)(2,1)} fusion(f32[3,6,128,128]{3,2,1,0:T(8,128)S(1)} %copy-done.9, bf16[3,6,128,128]{3,2,1,0:T(8,128)(2,1)S(1)} %add_convert_fusion, bf16[3,128,6,128]{1,3,2,0:T(8,128)(2,1)S(1)} %bitcast.78), kind=kOutput, calls=%fused_computation.27 | convolution fusion | flops 76382208 | bytes 2949120 | tf_op jit(solution)/shard_map/nshe,nhde->nshd/dot_general | solution.py:121
  40.0 2.4 %copy.70 = bf16[3,128,6,128]{3,2,1,0:T(8,128)(2,1)} copy(bf16[3,128,6,128]{1,3,2,0:T(8,128)(2,1)} %fusion.14) | data formatting | bytes 1179648 | tf_op jit(solution)/shard_map/mul | solution.py:119
  42.4 2.5 %stack.13 = bf16[1,1,384,768]{3,2,1,0:T(8,128)(2,1)} reshape(bf16[3,128,6,128]{3,2,1,0:T(8,128)(2,1)} %copy.70) | data formatting | bytes 1179648 | tf_op jit(solution)/shard_map/stack | solution.py:128
  44.8 0.0 copy-done.6
  44.8 0.3 fusion.34
  45.1 0.7 copy-done.2
  45.9 0.2 copy-done.8
  46.1 1.2 %fusion.13 = bf16[3,128,6,128]{1,3,2,0:T(8,128)(2,1)} fusion(f32[3,6,128,128]{3,2,1,0:T(8,128)S(1)} %fusion.34, bf16[3,6,128,128]{3,2,1,0:T(8,128)(2,1)S(1)} %copy-done.8, bf16[3,128,6,128]{1,3,2,0:T(8,128)(2,1)S(1)} %bitcast.83), kind=kOutput, calls=%fused_computation.26 | convolution fusion | flops 76382208 | bytes 2949120 | tf_op jit(solution)/shard_map/nshd,nhde->nshe/dot_general | solution.py:125
  47.3 2.3 %copy.75 = bf16[3,128,6,128]{3,2,1,0:T(8,128)(2,1)} copy(bf16[3,128,6,128]{1,3,2,0:T(8,128)(2,1)} %fusion.13) | data formatting | bytes 1179648 | tf_op jit(solution)/shard_map/mul | solution.py:123
  49.6 2.5 %stack.14 = bf16[1,1,384,768]{3,2,1,0:T(8,128)(2,1)} reshape(bf16[3,128,6,128]{3,2,1,0:T(8,128)(2,1)} %copy.75) | data formatting | bytes 1179648 | tf_op jit(solution)/shard_map/stack | solution.py:128
  52.0 2.6 %fusion.15 = bf16[3,128,6,128]{1,3,2,0:T(8,128)(2,1)} fusion(f32[3,6,128,128]{3,2,1,0:T(8,128)} %fusion.32, bf16[3,128,6,128]{1,3,2,0:T(8,128)(2,1)S(1)} %multiply_convert_fusion, f32[2,6,128,128]{3,2,1,0:T(8,128)} %slice.8, f32[6,128,128]{2,1,0:T(8,128)S(1)} %get-tuple-element.81), kind=kOutput, calls=%fused_computation.28 | convolution fusion | flops 76972032 | bytes 3538944 | tf_op jit(solution)/shard_map/nthe,nhde->nthd/dot_general | solution.py:117
  54.7 2.4 %copy.65 = bf16[3,128,6,128]{3,2,1,0:T(8,128)(2,1)} copy(bf16[3,128,6,128]{1,3,2,0:T(8,128)(2,1)} %fusion.15) | data formatting | bytes 1179648 | tf_op jit(solution)/shard_map/mul | solution.py:115
  57.0 2.5 %stack.12 = bf16[1,1,384,768]{3,2,1,0:T(8,128)(2,1)} reshape(bf16[3,128,6,128]{3,2,1,0:T(8,128)(2,1)} %copy.65) | data formatting | bytes 1179648 | tf_op jit(solution)/shard_map/stack | solution.py:128
  59.5 0.0 copy-done.10
  59.5 1.4 %pad_maximum_fusion = bf16[1,3,384,768]{3,2,1,0:T(8,128)(2,1)S(1)} fusion(bf16[1,1,384,768]{3,2,1,0:T(8,128)(2,1)} %stack.14, bf16[1,1,384,768]{3,2,1,0:T(8,128)(2,1)S(1)} %copy-done.10, bf16[1,1,384,768]{3,2,1,0:T(8,128)(2,1)} %stack.12), kind=kLoop, calls=%fused_computation.2 | loop fusion | flops 1769472 | bytes 3538944 | tf_op jit(solution)/shard_map/stack | solution.py:128
  61.0 3.6 %collective-permute-start = (bf16[1,3,384,768]{3,2,1,0:T(8,128)(2,1)S(1)}, bf16[1,3,384,768]{3,2,1,0:T(8,128)(2,1)S(1)}, u32[]{:S(2)}, u32[]{:S(2)}) collective-permute-start(bf16[1,3,384,768]{3,2,1,0:T(8,128)(2,1)S(1)} %pad_maximum_fusion), channel_id=1, source_target_pairs={{0,12},{4,0},{8,4},{12,8},{1,13},{5,1},{9,5},{13,9},{2,14},{6,2},{... | collective-permute-start | bytes 5308424 | tf_op jit(solution)/shard_map/ppermute | solution.py:35
  64.6 0.5 fusion.35
  65.1 0.0 copy-done.5
  65.1 0.5 fusion.12
  65.6 1.6 %collective-permute-start.1 = (f32[384]{0:T(512)S(1)}, f32[384]{0:T(512)S(1)}, u32[]{:S(2)}, u32[]{:S(2)}) collective-permute-start(f32[384]{0:T(512)S(1)} %bitcast.89), channel_id=1, source_target_pairs={{0,1},{1,0},{2,3},{3,2},{4,5},{5,4},{6,7},{7,6},{8,9},{9,8},{10,11... | collective-permute-start | bytes 4616 | tf_op jit(solution)/shard_map/ppermute | solution.py:15
  67.2 2.0 %collective-permute-done.1 = f32[384]{0:T(512)S(1)} collective-permute-done((f32[384]{0:T(512)S(1)}, f32[384]{0:T(512)S(1)}, u32[]{:S(2)}, u32[]{:S(2)}) %collective-permute-start.1) | collective-permute-done | bytes 1568 | tf_op jit(solution)/shard_map/ppermute | solution.py:15
  69.2 2.6 %collective-permute-start.2 = (f32[384]{0:T(512)S(1)}, f32[384]{0:T(512)S(1)}, u32[]{:S(2)}, u32[]{:S(2)}) collective-permute-start(f32[384]{0:T(512)S(1)} %bitcast_add_fusion.2), channel_id=1, source_target_pairs={{0,2},{1,3},{2,0},{3,1},{4,6},{5,7},{6,4},{7,5},{8,10},{9,11},{10,... | collective-permute-start | bytes 4616 | tf_op jit(solution)/shard_map/ppermute | solution.py:15
  71.8 1.9 %collective-permute-done.2 = f32[384]{0:T(512)S(1)} collective-permute-done((f32[384]{0:T(512)S(1)}, f32[384]{0:T(512)S(1)}, u32[]{:S(2)}, u32[]{:S(2)}) %collective-permute-start.2) | collective-permute-done | bytes 1568 | tf_op jit(solution)/shard_map/ppermute | solution.py:15
  73.7 0.6 reshape.92
  74.3 27.6 %collective-permute-done = bf16[1,3,384,768]{3,2,1,0:T(8,128)(2,1)S(1)} collective-permute-done((bf16[1,3,384,768]{3,2,1,0:T(8,128)(2,1)S(1)}, bf16[1,3,384,768]{3,2,1,0:T(8,128)(2,1)S(1)}, u32[]{:S(2)}, u32[]{:S(2)}) %collective-permute-start) | collective-permute-done | bytes 1769504 | tf_op jit(solution)/shard_map/ppermute | solution.py:35
  101.9 1.2 %copy.113 = bf16[1,3,384,768]{3,2,1,0:T(8,128)(2,1)} copy(bf16[1,3,384,768]{3,2,1,0:T(8,128)(2,1)S(1)} %collective-permute-done) | data formatting | bytes 3538944
  (20 shorter events, 0.1 us)
Async XLA Ops:
  0.6 1.5 %copy-start = (bf16[1,512,768]{2,1,0:T(8,128)(2,1)S(1)}, bf16[1,512,768]{2,1,0:T(8,128)(2,1)}, u32[]{:S(2)}) copy-start(bf16[1,512,768]{2,1,0:T(8,128)(2,1)} %param.11) | copy-start | bytes 2359300
  5.9 15.9 %copy-start.1 = (bf16[3,128,768]{1,2,0:T(8,128)(2,1)}, bf16[3,128,768]{1,2,0:T(8,128)(2,1)S(1)}, u32[]{:S(2)}) copy-start(bf16[3,128,768]{1,2,0:T(8,128)(2,1)S(1)} %copy.56) | copy-start | bytes 1769476
  5.9 4.5 %copy-start.12 = (bf16[1,512,768]{2,1,0:T(8,128)(2,1)S(1)}, bf16[1,512,768]{2,1,0:T(8,128)(2,1)}, u32[]{:S(2)}) copy-start(bf16[1,512,768]{2,1,0:T(8,128)(2,1)} %param.14) | copy-start | bytes 2359300
  12.3 2.5 %copy-start.13 = (f32[1,512]{1,0:T(1,128)S(1)}, f32[1,512]{1,0:T(1,128)}, u32[]{:S(2)}) copy-start(f32[1,512]{1,0:T(1,128)} %param.15) | copy-start | bytes 6148
  16.4 1.3 %copy-start.3 = (f32[3,128,768]{1,2,0:T(8,128)S(1)}, f32[3,128,768]{1,2,0:T(8,128)}, u32[]{:S(2)}) copy-start(f32[3,128,768]{1,2,0:T(8,128)} %copy.58) | copy-start | bytes 3538948
  27.4 1.1 %copy-start.11 = (f32[6,128,128]{2,1,0:T(8,128)S(1)}, f32[6,128,128]{2,1,0:T(8,128)}, u32[]{:S(2)}) copy-start(f32[6,128,128]{2,1,0:T(8,128)} %get-tuple-element.99) | copy-start | bytes 1179652
  37.4 1.5 %copy-start.9 = (f32[3,6,128,128]{3,2,1,0:T(8,128)S(1)}, f32[3,6,128,128]{3,2,1,0:T(8,128)}, u32[]{:S(2)}) copy-start(f32[3,6,128,128]{3,2,1,0:T(8,128)} %fusion.33) | copy-start | bytes 3538948
  37.5 0.8 copy-start.7
  40.0 4.8 %copy-start.6 = (bf16[3,6,128,128]{3,2,1,0:T(8,128)(2,1)S(1)}, bf16[3,6,128,128]{3,2,1,0:T(8,128)(2,1)}, u32[]{:S(2)}) copy-start(bf16[3,6,128,128]{3,2,1,0:T(8,128)(2,1)} %fusion.10) | copy-start | bytes 1769476
  44.8 1.1 %copy-start.2 = (bf16[3,128,768]{1,2,0:T(8,128)(2,1)S(1)}, bf16[3,128,768]{1,2,0:T(8,128)(2,1)}, u32[]{:S(2)}) copy-start(bf16[3,128,768]{1,2,0:T(8,128)(2,1)} %copy-done.1) | copy-start | bytes 1769476
  44.8 1.2 %copy-start.8 = (bf16[3,6,128,128]{3,2,1,0:T(8,128)(2,1)S(1)}, bf16[3,6,128,128]{3,2,1,0:T(8,128)(2,1)}, u32[]{:S(2)}) copy-start(bf16[3,6,128,128]{3,2,1,0:T(8,128)(2,1)} %copy-done.7) | copy-start | bytes 1769476
  54.7 4.8 %copy-start.10 = (bf16[1,1,384,768]{3,2,1,0:T(8,128)(2,1)S(1)}, bf16[1,1,384,768]{3,2,1,0:T(8,128)(2,1)}, u32[]{:S(2)}) copy-start(bf16[1,1,384,768]{3,2,1,0:T(8,128)(2,1)} %stack.13) | copy-start | bytes 1769476
  60.9 4.2 %copy-start.4 = (f32[3,128,768]{1,2,0:T(8,128)S(1)}, f32[3,128,768]{1,2,0:T(8,128)}, u32[]{:S(2)}) copy-start(f32[3,128,768]{1,2,0:T(8,128)} %copy.58) | copy-start | bytes 3538948
  61.0 4.2 %copy-start.5 = (f32[2,6,128,128]{3,2,1,0:T(8,128)S(1)}, f32[2,6,128,128]{3,2,1,0:T(8,128)}, u32[]{:S(2)}) copy-start(f32[2,6,128,128]{3,2,1,0:T(8,128)} %slice.8) | copy-start | bytes 2359300
  61.0 40.9 %collective-permute-start = (bf16[1,3,384,768]{3,2,1,0:T(8,128)(2,1)S(1)}, bf16[1,3,384,768]{3,2,1,0:T(8,128)(2,1)S(1)}, u32[]{:S(2)}, u32[]{:S(2)}) collective-permute-start(bf16[1,3,384,768]{3,2,1,0:T(8,128)(2,1)S(1)} %pad_maximum_fusion), channel_id=1, source_target_pairs={{0,12},{4,0},{8,4},{12,8},{1,13},{5,1},{9,5},{13,9},{2,14},{6,2},{... | collective-permute-start | bytes 5308424 | tf_op jit(solution)/shard_map/ppermute | solution.py:35
  65.6 3.6 %collective-permute-start.1 = (f32[384]{0:T(512)S(1)}, f32[384]{0:T(512)S(1)}, u32[]{:S(2)}, u32[]{:S(2)}) collective-permute-start(f32[384]{0:T(512)S(1)} %bitcast.89), channel_id=1, source_target_pairs={{0,1},{1,0},{2,3},{3,2},{4,5},{5,4},{6,7},{7,6},{8,9},{9,8},{10,11... | collective-permute-start | bytes 4616 | tf_op jit(solution)/shard_map/ppermute | solution.py:15
  69.2 4.5 %collective-permute-start.2 = (f32[384]{0:T(512)S(1)}, f32[384]{0:T(512)S(1)}, u32[]{:S(2)}, u32[]{:S(2)}) collective-permute-start(f32[384]{0:T(512)S(1)} %bitcast_add_fusion.2), channel_id=1, source_target_pairs={{0,2},{1,3},{2,0},{3,1},{4,6},{5,7},{6,4},{7,5},{8,10},{9,11},{10,... | collective-permute-start | bytes 4616 | tf_op jit(solution)/shard_map/ppermute | solution.py:15
